TPU v7x, 32 devices: a whole 2x2x4 slice. The times are simulated.
32 devices in a mesh: ctx: 8 (over z, x), tp: 4 (over y, core).
Axes of the slice: x: 2, y: 2, z: 4, core: 2. Of those that a mesh axis runs over, the one named last changes fastest.
Arguments:
- queries: bfloat16 [2048, 2560], P('ctx', 'tp'), may hold values from -5 to 5
- keys: bfloat16 [2048, 2560], P('ctx', 'tp'), may hold values from -5 to 5
- values: bfloat16 [2048, 2560], P('ctx', 'tp'), may hold values from -6 to 6
- block_mask: int32 [16, 16], replicated, may hold values from 0 to 1, as said below
- w_out: bfloat16 [2560, 5120], P('tp'), may hold values from -0.125 to 0.125
Outputs:
- mixed: bfloat16 [2048, 5120], P('ctx', 'tp')
Inputs may be any that keep to these rules, and one draw needn't show every extreme that they name: block_mask[b, b] = 1 for every block b. block_mask[i, j] = 0 whenever the ctx indices i // 2 and j // 2 differ by more than 2; where they differ by exactly 2 and i and j have the same position within their devices, block_mask[i, j] = 1.
All inputs are finite; a program needn't handle non-finite values.
Results may differ from a plain program's by a relative error of at most 0.014.
Values may be sent and summed in bfloat16 or wider, within the bound.
A program may use at most 64 MiB of HBM per device.

v0:
```python
import jax
import jax.numpy as jnp
from jax import lax
from jax.sharding import PartitionSpec as P

HD = 128
BLK = 128


def from_behind(value, axis, by):
    count = lax.axis_size(axis)
    pairs = [(i, i + by) for i in range(count) if 0 <= i + by < count]
    return lax.ppermute(value, axis, pairs)


def expand_blocks(columns):
    return jnp.repeat(jnp.repeat(columns, BLK, axis=0), BLK, axis=1) > 0


def attend_piece(carry, query_heads, key_piece, value_piece, columns):
    running_max, running_sum, accumulated = carry
    count = key_piece.shape[0]
    head_count = query_heads.shape[1]
    key_heads = key_piece.reshape(count, head_count, HD)
    value_heads = value_piece.reshape(count, head_count, HD)
    allowed = expand_blocks(columns)[None, :, :]
    scores = jnp.einsum(
        "thd,shd->hts", query_heads, key_heads, preferred_element_type=jnp.float32
    ) * HD ** (-0.5)
    masked = jnp.where(allowed, scores, jnp.float32(-1e30))
    new_max = jnp.maximum(running_max, jnp.max(masked, axis=2))
    weights = jnp.where(allowed, jnp.exp(masked - new_max[:, :, None]), jnp.float32(0.0))
    factor = jnp.exp(running_max - new_max)
    new_sum = running_sum * factor + jnp.sum(weights, axis=2)
    product = jnp.einsum(
        "hts,shd->htd",
        weights.astype(jnp.bfloat16),
        value_heads,
        preferred_element_type=jnp.float32,
    )
    return (new_max, new_sum, accumulated * factor[:, :, None] + product)


def shards(queries, keys, values, block_mask, w_out):
    tok_rows = queries.shape[0]
    head_count = queries.shape[1] // HD
    per_dev = tok_rows // BLK
    position = lax.axis_index("ctx")
    reach = lax.axis_size("ctx") // 4
    own_rows = lax.dynamic_slice_in_dim(block_mask, position * per_dev, per_dev, 0)
    padded_rows = jnp.pad(own_rows, ((0, 0), (reach * per_dev, reach * per_dev)))
    query_heads = queries.reshape(tok_rows, head_count, HD)
    start_max = jnp.full((head_count, tok_rows), -1e30, jnp.float32)
    start_sum = jnp.zeros((head_count, tok_rows), jnp.float32)
    start_acc = jnp.zeros((head_count, tok_rows, HD), jnp.float32)
    stacked = jnp.stack([keys, values])

    def columns_at(offset):
        return lax.dynamic_slice_in_dim(
            padded_rows, (position + offset + reach) * per_dev, per_dev, 1
        )

    carry = attend_piece(
        (start_max, start_sum, start_acc), query_heads, keys, values, columns_at(0)
    )
    turn_ids = jnp.arange(1, reach + 1, dtype=jnp.int32)

    def forward_step(state, turn):
        inner, moving = state
        moving = from_behind(moving, "ctx", 1)
        inner = attend_piece(inner, query_heads, moving[0], moving[1], columns_at(-turn))
        return ((inner, moving), None)

    def backward_step(state, turn):
        inner, moving = state
        moving = from_behind(moving, "ctx", -1)
        inner = attend_piece(inner, query_heads, moving[0], moving[1], columns_at(turn))
        return ((inner, moving), None)

    (carry, unused_one), unused = lax.scan(forward_step, (carry, stacked), turn_ids)
    (carry, unused_two), unused = lax.scan(backward_step, (carry, stacked), turn_ids)
    final_max, totals, accumulated = carry
    heads_out = accumulated / totals[:, :, None]
    attended = (
        jnp.transpose(heads_out, (1, 0, 2)).reshape(tok_rows, head_count * HD).astype(jnp.bfloat16)
    )
    partial_out = jnp.dot(attended, w_out, preferred_element_type=jnp.float32)
    return lax.psum_scatter(partial_out.astype(jnp.bfloat16), "tp", scatter_dimension=1, tiled=True)


def solution(mesh):
    return jax.shard_map(
        shards,
        mesh=mesh,
        in_specs=(P("ctx", "tp"), P("ctx", "tp"), P("ctx", "tp"), P(), P("tp", None)),
        out_specs=P("ctx", "tp"),
        check_vma=False,
    )
```

profile of v0, /device:TPU:16, one launch (start us, length us, event | category | flops | bytes accessed | tf_op | source)
XLA Modules:
  0.0 140.1 jit_solution(591878004495883046)
XLA Ops:
  6.5 0.7 copy-done
  7.2 0.1 copy.41
  7.4 0.1 broadcast_bitcast_fusion.2
  7.4 1.1 copy.20
  8.6 1.1 copy.19
  9.7 0.2 copy.28
  10.0 0.4 fusion.30
  10.4 0.2 fusion.18
  10.7 0.3 copy-done.1
  10.9 0.2 copy.23
  11.1 0.1 pad_maximum_fusion
  11.2 0.8 copy.59
  12.0 0.6 convolution_add_fusion.2
  12.6 42.7 %while.32 = (s32[]{:T(128)}, f32[5,256]{1,0:T(8,128)S(1)}, f32[5,256]{1,0:T(8,128)S(1)}, f32[5,256,128]{2,1,0:T(8,128)S(1)}, bf16[2,256,640]{1,2,0:T(8,128)(2,1)...) while((s32[]{:T(128)}, f32[5,256]{1,0:T(8,128)S(1)}, ...), condition=%wide.region_5.6_spmd, body=%wide.region_2.5_spmd.sunk | while | flops 171051536 | bytes 11815195 | solution.py:80
  12.6 3.4 %collective-permute-start = (bf16[2,256,640]{1,2,0:T(8,128)(2,1)}, bf16[2,256,640]{1,2,0:T(8,128)(2,1)S(1)}, u32[]{:S(2)}, u32[]{:S(2)}) collective-permute-start(bf16[2,256,640]{1,2,0:T(8,128)(2,1)} %get-tuple-element.328), channel_id=1, source_target_pairs={{0,4},{4,8},{8,12},{12,16},{16,20},{20,24},{24,28},{1,5},{5,9},{9,... | collective-permute-start | bytes 1966088 | tf_op jit(solution)/shard_map/while/body/eval_jaxpr/ppermute | solution.py:13
  16.0 0.6 dynamic_slice.32
  17.3 0.1 broadcast_bitcast_fusion.5
  17.4 14.7 %collective-permute-done = bf16[2,256,640]{1,2,0:T(8,128)(2,1)S(1)} collective-permute-done((bf16[2,256,640]{1,2,0:T(8,128)(2,1)}, bf16[2,256,640]{1,2,0:T(8,128)(2,1)S(1)}, u32[]{:S(2)}, u32[]{:S(2)}) %collective-permute-start) | collective-permute-done | bytes 655392 | tf_op jit(solution)/shard_map/while/body/eval_jaxpr/ppermute | solution.py:13
  32.2 0.4 fusion.61
  32.6 0.2 fusion.62
  32.9 0.6 convolution_add_fusion.5
  33.5 0.8 copy.69
  34.4 2.5 %collective-permute-start = (bf16[2,256,640]{1,2,0:T(8,128)(2,1)}, bf16[2,256,640]{1,2,0:T(8,128)(2,1)S(1)}, u32[]{:S(2)}, u32[]{:S(2)}) collective-permute-start(bf16[2,256,640]{1,2,0:T(8,128)(2,1)} %get-tuple-element.328), channel_id=1, source_target_pairs={{0,4},{4,8},{8,12},{12,16},{16,20},{20,24},{24,28},{1,5},{5,9},{9,... | collective-permute-start | bytes 1966088 | tf_op jit(solution)/shard_map/while/body/eval_jaxpr/ppermute | solution.py:13
  36.9 0.6 dynamic_slice.32
  38.2 0.1 broadcast_bitcast_fusion.5
  38.2 14.7 %collective-permute-done = bf16[2,256,640]{1,2,0:T(8,128)(2,1)S(1)} collective-permute-done((bf16[2,256,640]{1,2,0:T(8,128)(2,1)}, bf16[2,256,640]{1,2,0:T(8,128)(2,1)S(1)}, u32[]{:S(2)}, u32[]{:S(2)}) %collective-permute-start) | collective-permute-done | bytes 655392 | tf_op jit(solution)/shard_map/while/body/eval_jaxpr/ppermute | solution.py:13
  53.1 0.4 fusion.61
  53.5 0.2 fusion.62
  53.8 0.6 convolution_add_fusion.5
  54.4 0.8 copy.69
  55.3 35.5 %while.33 = (s32[]{:T(128)}, f32[5,256]{1,0:T(8,128)S(1)}, f32[5,256]{1,0:T(8,128)S(1)}, f32[5,256,128]{2,1,0:T(8,128)S(1)}, bf16[2,256,640]{1,2,0:T(8,128)(2,1)...) while((s32[]{:T(128)}, f32[5,256]{1,0:T(8,128)S(1)}, ...), condition=%wide.region_9.10_spmd, body=%wide.region_6.9_spmd.sunk | while | flops 171051520 | bytes 11815187 | solution.py:81
  55.3 1.9 %collective-permute-start.1 = (bf16[2,256,640]{1,2,0:T(8,128)(2,1)S(1)}, bf16[2,256,640]{1,2,0:T(8,128)(2,1)S(1)}, u32[]{:S(2)}, u32[]{:S(2)}) collective-permute-start(bf16[2,256,640]{1,2,0:T(8,128)(2,1)S(1)} %get-tuple-element.367), channel_id=1, source_target_pairs={{4,0},{8,4},{12,8},{16,12},{20,16},{24,20},{28,24},{5,1},{9,5},{13... | collective-permute-start | bytes 1966088 | tf_op jit(solution)/shard_map/while/body/eval_jaxpr/ppermute | solution.py:13
  57.2 0.6 dynamic_slice.34
  58.5 0.1 broadcast_bitcast_fusion.6
  58.5 13.4 %collective-permute-done.1 = bf16[2,256,640]{1,2,0:T(8,128)(2,1)S(1)} collective-permute-done((bf16[2,256,640]{1,2,0:T(8,128)(2,1)S(1)}, bf16[2,256,640]{1,2,0:T(8,128)(2,1)S(1)}, u32[]{:S(2)}, u32[]{:S(2)}) %collective-permute-start.1) | collective-permute-done | bytes 655392 | tf_op jit(solution)/shard_map/while/body/eval_jaxpr/ppermute | solution.py:13
  72.0 0.4 fusion.68
  72.4 0.2 fusion.69
  72.7 0.7 convolution_add_fusion.6
  73.4 3.1 %collective-permute-start.1 = (bf16[2,256,640]{1,2,0:T(8,128)(2,1)S(1)}, bf16[2,256,640]{1,2,0:T(8,128)(2,1)S(1)}, u32[]{:S(2)}, u32[]{:S(2)}) collective-permute-start(bf16[2,256,640]{1,2,0:T(8,128)(2,1)S(1)} %get-tuple-element.367), channel_id=1, source_target_pairs={{4,0},{8,4},{12,8},{16,12},{20,16},{24,20},{28,24},{5,1},{9,5},{13... | collective-permute-start | bytes 1966088 | tf_op jit(solution)/shard_map/while/body/eval_jaxpr/ppermute | solution.py:13
  76.5 0.6 dynamic_slice.34
  77.8 0.1 broadcast_bitcast_fusion.6
  77.9 11.3 %collective-permute-done.1 = bf16[2,256,640]{1,2,0:T(8,128)(2,1)S(1)} collective-permute-done((bf16[2,256,640]{1,2,0:T(8,128)(2,1)S(1)}, bf16[2,256,640]{1,2,0:T(8,128)(2,1)S(1)}, u32[]{:S(2)}, u32[]{:S(2)}) %collective-permute-start.1) | collective-permute-done | bytes 655392 | tf_op jit(solution)/shard_map/while/body/eval_jaxpr/ppermute | solution.py:13
  89.3 0.4 fusion.68
  89.8 0.2 fusion.69
  90.0 0.7 convolution_add_fusion.6
  90.8 0.2 copy.30
  91.1 6.6 %convolution_convert_fusion = bf16[256,5120]{1,0:T(8,128)(2,1)} fusion(bf16[256,640]{0,1:T(8,128)(2,1)S(1)} %bitcast.101, bf16[640,5120]{1,0:T(8,128)(2,1)} %param.13), kind=kOutput, calls=%fused_computation.30 | convolution fusion | flops 1679032320 | bytes 9502720 | tf_op jit(solution)/shard_map/dot_general | solution.py:87
  97.7 35.6 %reduce-scatter.2.cloned.1.call-done = bf16[256,1280]{1,0:T(8,128)(2,1)} async-done(((bf16[256,5120]{1,0:T(8,128)(2,1)}), bf16[256,1280]{1,0:T(8,128)(2,1)}) %reduce-scatter.2.cloned.1.call-update) | async-done | bytes 655376 | tf_op jit(solution)/shard_map/reduce_scatter | solution.py:88
  (43 shorter events, 0.7 us)
Async XLA Ops:
  6.5 0.7 copy-start
  6.5 126.7 %reduce-scatter.2.cloned.1.call-start = ((), (), s32[]{:S(2)}) async-start(), calls=%async_computation.1 | async-start | bytes 3276800 | tf_op jit(solution)/shard_map/reduce_scatter | solution.py:88
  10.0 1.0 copy-start.1
  12.6 19.5 %collective-permute-start = (bf16[2,256,640]{1,2,0:T(8,128)(2,1)}, bf16[2,256,640]{1,2,0:T(8,128)(2,1)S(1)}, u32[]{:S(2)}, u32[]{:S(2)}) collective-permute-start(bf16[2,256,640]{1,2,0:T(8,128)(2,1)} %get-tuple-element.328), channel_id=1, source_target_pairs={{0,4},{4,8},{8,12},{12,16},{16,20},{20,24},{24,28},{1,5},{5,9},{9,... | collective-permute-start | bytes 1966088 | tf_op jit(solution)/shard_map/while/body/eval_jaxpr/ppermute | solution.py:13
  34.4 18.6 %collective-permute-start = (bf16[2,256,640]{1,2,0:T(8,128)(2,1)}, bf16[2,256,640]{1,2,0:T(8,128)(2,1)S(1)}, u32[]{:S(2)}, u32[]{:S(2)}) collective-permute-start(bf16[2,256,640]{1,2,0:T(8,128)(2,1)} %get-tuple-element.328), channel_id=1, source_target_pairs={{0,4},{4,8},{8,12},{12,16},{16,20},{20,24},{24,28},{1,5},{5,9},{9,... | collective-permute-start | bytes 1966088 | tf_op jit(solution)/shard_map/while/body/eval_jaxpr/ppermute | solution.py:13
  55.3 16.6 %collective-permute-start.1 = (bf16[2,256,640]{1,2,0:T(8,128)(2,1)S(1)}, bf16[2,256,640]{1,2,0:T(8,128)(2,1)S(1)}, u32[]{:S(2)}, u32[]{:S(2)}) collective-permute-start(bf16[2,256,640]{1,2,0:T(8,128)(2,1)S(1)} %get-tuple-element.367), channel_id=1, source_target_pairs={{4,0},{8,4},{12,8},{16,12},{20,16},{24,20},{28,24},{5,1},{9,5},{13... | collective-permute-start | bytes 1966088 | tf_op jit(solution)/shard_map/while/body/eval_jaxpr/ppermute | solution.py:13
  73.4 15.8 %collective-permute-start.1 = (bf16[2,256,640]{1,2,0:T(8,128)(2,1)S(1)}, bf16[2,256,640]{1,2,0:T(8,128)(2,1)S(1)}, u32[]{:S(2)}, u32[]{:S(2)}) collective-permute-start(bf16[2,256,640]{1,2,0:T(8,128)(2,1)S(1)} %get-tuple-element.367), channel_id=1, source_target_pairs={{4,0},{8,4},{12,8},{16,12},{20,16},{24,20},{28,24},{5,1},{9,5},{13... | collective-permute-start | bytes 1966088 | tf_op jit(solution)/shard_map/while/body/eval_jaxpr/ppermute | solution.py:13
Sparse Core Ops, SparseCore 0:
  97.8 35.4 reduce-scatter.1
where the time goes:
time: 142 us; the launch traced here: 140 us
  waiting for transfers between devices  89.7 us (63%)
  between operations  13.5 us (10%)
  matrix products  11.9 us (8%)
  starting transfers between devices  10.9 us (8%)
  local copies, waits for them, and re-layouts  9.69 us (7%)
  loops' own time  2.94 us (2%)
  other arithmetic  1.49 us (1%)
    ppermute x4, waiting for transfers between devices, from_behind(): return lax.ppermute(value, axis, pairs)  54.2 us
    reduce_scatter x1, waiting for transfers between devices, shards(): lax.psum_scatter(partial_out.astype(jnp.bfloat16), 'tp', scatter_dimensio...  35.6 us
    ppermute x4, starting transfers between devices, from_behind(): return lax.ppermute(value, axis, pairs)  10.9 us
    dot_general x1, matrix products, shards(): partial_out = jnp.dot(attended, w_out, preferred_element_type=jnp.float32)  6.61 us
    unnamed x11, local copies, waits for them, and re-layouts  4.43 us
    dot_general x5, matrix products, attend_piece(): jnp.einsum('hts,shd->htd', weights.astype(jnp.bfloat16), value_heads, pre...  3.15 us
  transfers between devices with their start and end apart: 5, of which 5 were waited for; matrix products, arithmetic and copies ran while one was open for 2% of the time, Pallas kernels for 0%

commit v1 on v0

v1 whole, which is shorter than its diff:
```python
import functools
import math

import jax
import jax.numpy as jnp
from jax import lax
from jax.experimental import pallas as pl
from jax.experimental.pallas import tpu as pltpu
from jax.sharding import PartitionSpec as P

HD = 128
BLK = 128
MESH = pl.DeviceIdType.MESH
K, V = 0, 1


def kernel(
    reach, count, tp_count, chunks,
    mask_ref, q_ref, k_ref, v_ref, w_ref, out_ref,
    kv, w_vm, acc, peak, total, att, stage_p, recv_p, stage_y, recv_y, final,
    kv_local, w_local, own_send, relay_send, kv_recv, p_send, p_recv, y_send, y_recv,
):
    tok, cols = q_ref.shape
    heads = cols // HD
    per = tok // BLK
    chips = tp_count // 2
    out_cols = out_ref.shape[1]
    width = out_cols // chunks
    ctx = lax.axis_index("ctx")
    t = lax.axis_index("tp")
    inner = lax.rem(ctx, reach)
    core = lax.rem(t, 2)
    chip = t // 2
    partner = chip * 2 + 1 - core

    def tp_of(jy, which):
        return lax.rem(chip + jy, chips) * 2 + which

    def each_peer(fn):
        if reach == 2:
            fn(1)
        elif reach > 2:
            def step(j, carry):
                fn(j)
                return carry
            lax.fori_loop(1, reach, step, 0)

    def row_peer(j):
        return ctx - inner + lax.rem(inner + j, reach)

    def inside(c):
        return jnp.logical_and(c >= 0, c < count)

    own = [
        pltpu.make_async_copy(k_ref, kv.at[reach, K], kv_local.at[K]),
        pltpu.make_async_copy(v_ref, kv.at[reach, V], kv_local.at[V]),
    ]
    weights = [
        pltpu.make_async_copy(
            w_ref.at[:, s * out_cols:(s + 1) * out_cols], w_vm.at[s], w_local.at[s]
        )
        for s in range(tp_count)
    ]
    for copy in own:
        copy.start()

    barrier = pltpu.get_barrier_semaphore()

    def greet(c, tt):
        pl.semaphore_signal(barrier, inc=1, device_id=(c, tt), device_id_type=MESH)

    each_peer(lambda j: greet(row_peer(j), t))
    for away in (-reach, reach):
        @pl.when(inside(ctx + away))
        def _(away=away):
            greet(ctx + away, t)
    greet(ctx, partner)
    for jy in range(1, chips):
        greet(ctx, tp_of(jy, core))
    outer_count = inside(ctx - reach).astype(jnp.int32) + inside(ctx + reach).astype(jnp.int32)
    pl.semaphore_wait(barrier, reach - 1 + 1 + chips - 1 + outer_count)

    def own_copy(dest, half):
        return pltpu.make_async_remote_copy(
            src_ref=(k_ref, v_ref)[half],
            dst_ref=kv.at[ctx - dest + reach, half],
            send_sem=own_send.at[dest - ctx + reach, half],
            recv_sem=kv_recv.at[ctx - dest + reach, half],
            device_id=(dest, t),
            device_id_type=MESH,
        )

    def outer(fn):
        for away in (-reach, reach):
            @pl.when(inside(ctx + away))
            def _(away=away):
                fn(ctx + away)

    each_peer(lambda j: own_copy(row_peer(j), V).start())
    outer(lambda dest: own_copy(dest, K).start())
    each_peer(lambda j: own_copy(row_peer(j), K).start())
    outer(lambda dest: own_copy(dest, V).start())
    for copy in weights:
        copy.start()

    def wait_piece(src, half):
        slot = src - ctx + reach
        pltpu.make_async_remote_copy(
            src_ref=kv.at[slot, half],
            dst_ref=kv.at[slot, half],
            send_sem=own_send.at[slot, half],
            recv_sem=kv_recv.at[slot, half],
            device_id=(ctx, partner),
            device_id_type=MESH,
        ).wait_recv()

    def attend(src, first):
        slot = src - ctx + reach
        factor = jnp.float32(HD ** (-0.5) * math.log2(math.e))
        bias_rows = []
        for a in range(per):
            parts = []
            for b in range(per):
                flag = mask_ref[ctx * per + a, src * per + b]
                value = jnp.where(flag > 0, jnp.float32(0.0), jnp.float32(-1e30))
                parts.append(jnp.full((1, BLK), value, jnp.float32))
            bias_rows.append(jnp.concatenate(parts, axis=1))
        for h in range(heads):
            lanes = slice(h * HD, (h + 1) * HD)
            key = kv[slot, K, :, lanes]
            value = kv[slot, V, :, lanes]
            for a in range(per):
                rows = slice(a * BLK, (a + 1) * BLK)
                scores = lax.dot_general(
                    q_ref[rows, lanes], key, (((1,), (1,)), ((), ())),
                    preferred_element_type=jnp.float32,
                ) + bias_rows[a]
                top = jnp.max(scores, axis=1, keepdims=True)
                if not first:
                    before = peak[h, rows, 0:1]
                    top = jnp.maximum(before, top)
                weight = jnp.exp2((scores - top) * factor)
                summed = jnp.sum(weight, axis=1, keepdims=True)
                product = jnp.dot(
                    weight.astype(jnp.bfloat16), value, preferred_element_type=jnp.float32
                )
                if not first:
                    fade = jnp.exp2((before - top) * factor)
                    summed = summed + total[h, rows, 0:1] * fade
                    product = product + acc[rows, lanes] * fade
                peak[h, rows, :] = jnp.broadcast_to(top, (BLK, HD))
                total[h, rows, :] = jnp.broadcast_to(summed, (BLK, HD))
                acc[rows, lanes] = product

    for copy in own:
        copy.wait()
    attend(ctx, True)

    def value_relay(j):
        peer = row_peer(j)
        dest = jnp.where(peer > ctx, ctx + reach, ctx - reach)
        copy = pltpu.make_async_remote_copy(
            src_ref=kv.at[peer - ctx + reach, V],
            dst_ref=kv.at[peer - dest + reach, V],
            send_sem=relay_send.at[peer - ctx + reach, V],
            recv_sem=kv_recv.at[peer - dest + reach, V],
            device_id=(dest, t),
            device_id_type=MESH,
        )
        return inside(dest), copy

    def key_relay(j):
        peer = row_peer(j)
        src = jnp.where(peer < ctx, ctx - reach, ctx + reach)
        copy = pltpu.make_async_remote_copy(
            src_ref=kv.at[src - ctx + reach, K],
            dst_ref=kv.at[src - peer + reach, K],
            send_sem=relay_send.at[peer - ctx + reach, K],
            recv_sem=kv_recv.at[src - peer + reach, K],
            device_id=(peer, t),
            device_id_type=MESH,
        )
        return inside(src), copy

    def start_relay(make, j):
        valid, copy = make(j)

        @pl.when(valid)
        def _():
            copy.start()

    def end_relay(make, j):
        valid, copy = make(j)

        @pl.when(valid)
        def _():
            copy.wait_send()

    def take_values(j):
        wait_piece(row_peer(j), V)
        start_relay(value_relay, j)

    each_peer(take_values)
    outer(lambda src: wait_piece(src, K))
    each_peer(lambda j: start_relay(key_relay, j))

    def take_row(j):
        wait_piece(row_peer(j), K)
        attend(row_peer(j), False)

    each_peer(take_row)

    def take_outer(src):
        wait_piece(src, V)
        attend(src, False)

    outer(take_outer)

    def take_diagonal(j):
        peer = row_peer(j)
        src = jnp.where(peer > ctx, peer - reach, peer + reach)

        @pl.when(inside(src))
        def _():
            wait_piece(src, K)
            wait_piece(src, V)
            attend(src, False)

    each_peer(take_diagonal)

    for h in range(heads):
        lanes = slice(h * HD, (h + 1) * HD)
        att[:, lanes] = (acc[:, lanes] * (1.0 / total[h])).astype(jnp.bfloat16)
    for copy in weights:
        copy.wait()

    def project(slab, k):
        return jnp.dot(
            att[...], w_vm[slab, :, k * width:(k + 1) * width],
            preferred_element_type=jnp.float32,
        )

    def partner_copy(jy, k):
        return pltpu.make_async_remote_copy(
            src_ref=stage_p.at[jy, k],
            dst_ref=recv_p.at[jy, k],
            send_sem=p_send.at[jy, k],
            recv_sem=p_recv.at[jy, k],
            device_id=(ctx, partner),
            device_id_type=MESH,
        )

    def chip_copy(jy, k):
        return pltpu.make_async_remote_copy(
            src_ref=stage_y.at[jy, k],
            dst_ref=recv_y.at[chips - jy, k],
            send_sem=y_send.at[jy, k],
            recv_sem=y_recv.at[chips - jy, k],
            device_id=(ctx, tp_of(jy, core)),
            device_id_type=MESH,
        )

    pending = []

    def push(copy):
        while pending:
            pending.pop().start()
        if copy is not None:
            pending.append(copy)

    for jy in range(1, chips):
        for k in range(chunks):
            stage_p[jy, k] = project(tp_of(jy, 1 - core), k).astype(jnp.bfloat16)
            push(partner_copy(jy, k))
    for jy in range(1, chips):
        for k in range(chunks):
            mine = project(tp_of(jy, core), k)
            push(None)
            partner_copy(jy, k).wait_recv()
            stage_y[jy, k] = (mine + recv_p[jy, k].astype(jnp.float32)).astype(jnp.bfloat16)
            push(chip_copy(jy, k))
    for k in range(chunks):
        stage_p[0, k] = project(tp_of(0, 1 - core), k).astype(jnp.bfloat16)
        push(partner_copy(0, k))
    for k in range(chunks):
        mine = project(tp_of(0, core), k)
        push(None)
        partner_copy(0, k).wait_recv()
        final[k] = mine + recv_p[0, k].astype(jnp.float32)
    for k in range(chunks):
        result = final[k]
        for jy in range(1, chips):
            chip_copy(chips - jy, k).wait_recv()
            result = result + recv_y[jy, k].astype(jnp.float32)
        out_ref[:, k * width:(k + 1) * width] = result.astype(jnp.bfloat16)

    each_peer(lambda j: own_copy(row_peer(j), V).wait_send())
    each_peer(lambda j: own_copy(row_peer(j), K).wait_send())
    outer(lambda dest: own_copy(dest, K).wait_send())
    outer(lambda dest: own_copy(dest, V).wait_send())
    each_peer(lambda j: end_relay(value_relay, j))
    each_peer(lambda j: end_relay(key_relay, j))
    for jy in range(chips):
        for k in range(chunks):
            partner_copy(jy, k).wait_send()
    for jy in range(1, chips):
        for k in range(chunks):
            chip_copy(jy, k).wait_send()


def shards(count, tp_count, queries, keys, values, block_mask, w_out):
    tok, cols = queries.shape
    heads = cols // HD
    reach = count // 4
    chips = tp_count // 2
    depth, wide = w_out.shape
    out_cols = wide // tp_count
    chunks = max(1, out_cols // 256)
    width = out_cols // chunks
    bf16, f32 = jnp.bfloat16, jnp.float32
    dma = pltpu.SemaphoreType.DMA
    slots = 2 * reach + 1
    return pl.pallas_call(
        functools.partial(kernel, reach, count, tp_count, chunks),
        out_shape=jax.ShapeDtypeStruct((tok, out_cols), bf16),
        in_specs=[
            pl.BlockSpec(memory_space=pltpu.SMEM),
            pl.BlockSpec(memory_space=pltpu.VMEM),
            pl.BlockSpec(memory_space=pl.ANY),
            pl.BlockSpec(memory_space=pl.ANY),
            pl.BlockSpec(memory_space=pl.ANY),
        ],
        out_specs=pl.BlockSpec(memory_space=pltpu.VMEM),
        scratch_shapes=[
            pltpu.VMEM((slots, 2, tok, cols), bf16),
            pltpu.VMEM((tp_count, depth, out_cols), bf16),
            pltpu.VMEM((tok, cols), f32),
            pltpu.VMEM((heads, tok, HD), f32),
            pltpu.VMEM((heads, tok, HD), f32),
            pltpu.VMEM((tok, cols), bf16),
            pltpu.VMEM((chips, chunks, tok, width), bf16),
            pltpu.VMEM((chips, chunks, tok, width), bf16),
            pltpu.VMEM((chips, chunks, tok, width), bf16),
            pltpu.VMEM((chips, chunks, tok, width), bf16),
            pltpu.VMEM((chunks, tok, width), f32),
            dma((2,)),
            dma((tp_count,)),
            dma((slots, 2)),
            dma((slots, 2)),
            dma((slots, 2)),
            dma((chips, chunks)),
            dma((chips, chunks)),
            dma((chips, chunks)),
            dma((chips, chunks)),
        ],
        compiler_params=pltpu.CompilerParams(
            collective_id=0, has_side_effects=True, vmem_limit_bytes=60 * 1024 * 1024
        ),
    )(block_mask, queries, keys, values, w_out)


def solution(mesh):
    return jax.shard_map(
        functools.partial(shards, mesh.shape["ctx"], mesh.shape["tp"]),
        mesh=mesh,
        in_specs=(P("ctx", "tp"), P("ctx", "tp"), P("ctx", "tp"), P(), P("tp", None)),
        out_specs=P("ctx", "tp"),
        check_vma=False,
    )
```

time: 142 us -> 55.5 us (0.39); the launches traced: 140 us -> 55.3 us
  waiting for transfers between devices: 89.7 us -> 0 us
  Pallas kernels: 0 us -> 53.3 us
  between operations: 13.5 us -> 0.01 us
  matrix products: 11.9 us -> 0 us
  starting transfers between devices: 10.9 us -> 0 us
  local copies, waits for them, and re-layouts: 9.69 us -> 1.97 us
  loops' own time: 2.94 us -> 0 us
  other arithmetic: 1.49 us -> 0 us
    ppermute x4 -> x0, waiting for transfers between devices: 54.2 us -> none  [from_behind(): return lax.ppermute(value, axis, pairs)]
    pallas_call x0 -> x1, Pallas kernels: none -> 53.3 us  [shards(): pl.pallas_call(functools.partial(kernel, reach, count, tp_count, chunks),...]
    reduce_scatter x1 -> x0, waiting for transfers between devices: 35.6 us -> none  [shards(): lax.psum_scatter(partial_out.astype(jnp.bfloat16), 'tp', scatter_dimensio...]
    dot_general x11 -> x0, matrix products: 11.9 us -> none  [the longest x1 6.61 us: shards(): partial_out = jnp.dot(attended, w_out, preferred_element_type=jnp.float32)]
    ppermute x4 -> x0, starting transfers between devices: 10.9 us -> none  [from_behind(): return lax.ppermute(value, axis, pairs)]
    another operation x2 -> x0, loops' own time: 2.94 us -> none  [the longest x1 1.48 us: shards(): lax.scan(backward_step, (carry, stacked), turn_ids)]
    while x18 -> x0, local copies, waits for them, and re-layouts: 2.55 us -> none
    unnamed x11 -> x1, local copies, waits for them, and re-layouts: 4.43 us -> 1.97 us
  transfers between devices with their start and end apart: 5 -> 0, of which waited for: 5 -> 0; matrix products, arithmetic and copies ran while one was open for 2% -> 0% of each run, Pallas kernels for 0% -> 0%
where the time goes in v1:
time: 55.5 us; the launch traced here: 55.3 us
  Pallas kernels  53.3 us (96%)
  local copies, waits for them, and re-layouts  1.97 us (4%)
    pallas_call x1, Pallas kernels, shards(): pl.pallas_call(functools.partial(kernel, reach, count, tp_count, chunks),...  53.3 us
    unnamed x1, local copies, waits for them, and re-layouts  1.97 us

profile of v1, /device:TPU:16, one launch (start us, length us, event | category | flops | bytes accessed | tf_op | source)
XLA Modules:
  0.0 55.3 jit_solution(3795875258255924234)
XLA Ops:
  0.0 53.3 %shard_map.55 = bf16[256,1280]{1,0:T(8,128)(2,1)} custom-call(s32[16,16]{1,0:T(8,128)} %mask_ref.1, bf16[256,640]{1,0:T(8,128)(2,1)} %q_ref.1, bf16[256,640]{1,0:T(8,128)(2,1)} %k_ref.1, bf16[256,640]{1,0:T(8,128)(2,1)} %v_ref.1, bf16[640,5120]{1,0:T(8,128)(2,1)} %w_ref.1), custom_call_target="tpu_custom_call" | custom-call | tf_op jit(solution)/shard_map/pallas_call | solution.py:323
  53.3 2.0 %copy.7 = bf16[256,1280]{1,0:T(8,128)(2,1)} copy(bf16[256,1280]{1,0:T(8,128)(2,1)} %shard_map.55) | data formatting | bytes 1310720

commit v2 on v1

--- a/solution.py
+++ b/solution.py
@@ -12,12 +12,13 @@
 BLK = 128
 MESH = pl.DeviceIdType.MESH
 K, V = 0, 1
+OUTER_FIRST, ROW_FIRST = 0, 1
 
 
 def kernel(
     reach, count, tp_count, chunks,
     mask_ref, q_ref, k_ref, v_ref, w_ref, out_ref,
-    kv, w_vm, acc, peak, total, att, stage_p, recv_p, stage_y, recv_y, final,
+    kv, w_vm, acc, peak, att, stage_p, recv_p, stage_y, recv_y, final,
     kv_local, w_local, own_send, relay_send, kv_recv, p_send, p_recv, y_send, y_recv,
 ):
     tok, cols = q_ref.shape
@@ -51,9 +52,16 @@
     def inside(c):
         return jnp.logical_and(c >= 0, c < count)
 
+    part_rows = tok // 2
+
+    def part_of(half, kind):
+        return (k_ref, v_ref)[kind].at[half * part_rows:(half + 1) * part_rows, :]
+
     own = [
-        pltpu.make_async_copy(k_ref, kv.at[reach, K], kv_local.at[K]),
-        pltpu.make_async_copy(v_ref, kv.at[reach, V], kv_local.at[V]),
+        pltpu.make_async_copy(
+            part_of(half, kind), kv.at[reach, half * 2 + kind], kv_local.at[half * 2 + kind]
+        )
+        for half in (0, 1) for kind in (K, V)
     ]
     weights = [
         pltpu.make_async_copy(
@@ -80,15 +88,31 @@
     outer_count = inside(ctx - reach).astype(jnp.int32) + inside(ctx + reach).astype(jnp.int32)
     pl.semaphore_wait(barrier, reach - 1 + 1 + chips - 1 + outer_count)
 
+    class Pair:
+        def __init__(self, make):
+            self.copies = [make(K), make(V)]
+
+        def start(self):
+            for copy in self.copies:
+                copy.start()
+
+        def wait_send(self):
+            for copy in self.copies:
+                copy.wait_send()
+
+        def wait_recv(self):
+            for copy in self.copies:
+                copy.wait_recv()
+
     def own_copy(dest, half):
-        return pltpu.make_async_remote_copy(
-            src_ref=(k_ref, v_ref)[half],
-            dst_ref=kv.at[ctx - dest + reach, half],
-            send_sem=own_send.at[dest - ctx + reach, half],
-            recv_sem=kv_recv.at[ctx - dest + reach, half],
+        return Pair(lambda kind: pltpu.make_async_remote_copy(
+            src_ref=part_of(half, kind),
+            dst_ref=kv.at[ctx - dest + reach, half * 2 + kind],
+            send_sem=own_send.at[dest - ctx + reach, half * 2 + kind],
+            recv_sem=kv_recv.at[ctx - dest + reach, half * 2 + kind],
             device_id=(dest, t),
             device_id_type=MESH,
-        )
+        ))
 
     def outer(fn):
         for away in (-reach, reach):
@@ -96,91 +120,96 @@
             def _(away=away):
                 fn(ctx + away)
 
-    each_peer(lambda j: own_copy(row_peer(j), V).start())
-    outer(lambda dest: own_copy(dest, K).start())
-    each_peer(lambda j: own_copy(row_peer(j), K).start())
-    outer(lambda dest: own_copy(dest, V).start())
+    each_peer(lambda j: own_copy(row_peer(j), ROW_FIRST).start())
+    outer(lambda dest: own_copy(dest, OUTER_FIRST).start())
+    each_peer(lambda j: own_copy(row_peer(j), OUTER_FIRST).start())
+    outer(lambda dest: own_copy(dest, ROW_FIRST).start())
     for copy in weights:
         copy.start()
 
     def wait_piece(src, half):
         slot = src - ctx + reach
-        pltpu.make_async_remote_copy(
-            src_ref=kv.at[slot, half],
-            dst_ref=kv.at[slot, half],
-            send_sem=own_send.at[slot, half],
-            recv_sem=kv_recv.at[slot, half],
+        Pair(lambda kind: pltpu.make_async_remote_copy(
+            src_ref=kv.at[slot, half * 2 + kind],
+            dst_ref=kv.at[slot, half * 2 + kind],
+            send_sem=own_send.at[slot, half * 2 + kind],
+            recv_sem=kv_recv.at[slot, half * 2 + kind],
             device_id=(ctx, partner),
             device_id_type=MESH,
-        ).wait_recv()
-
-    def attend(src, first):
+        )).wait_recv()
+
+    def attend(src, halves, first=False):
         slot = src - ctx + reach
         factor = jnp.float32(HD ** (-0.5) * math.log2(math.e))
+        half_blocks = per // 2
+        blocks = [half * half_blocks + b for half in halves for b in range(half_blocks)]
+        span = len(blocks) * BLK
         bias_rows = []
         for a in range(per):
             parts = []
-            for b in range(per):
+            for b in blocks:
                 flag = mask_ref[ctx * per + a, src * per + b]
                 value = jnp.where(flag > 0, jnp.float32(0.0), jnp.float32(-1e30))
                 parts.append(jnp.full((1, BLK), value, jnp.float32))
             bias_rows.append(jnp.concatenate(parts, axis=1))
+        ones = jnp.ones((span, HD), jnp.bfloat16)
         for h in range(heads):
             lanes = slice(h * HD, (h + 1) * HD)
-            key = kv[slot, K, :, lanes]
-            value = kv[slot, V, :, lanes]
+            key = jnp.concatenate([kv[slot, half * 2 + K, :, lanes] for half in halves], axis=0)
+            value = jnp.concatenate([kv[slot, half * 2 + V, :, lanes] for half in halves], axis=0)
+            raw = lax.dot_general(
+                q_ref[:, lanes], key, (((1,), (1,)), ((), ())),
+                preferred_element_type=jnp.float32,
+            )
+            weights_of, fades = [], []
             for a in range(per):
                 rows = slice(a * BLK, (a + 1) * BLK)
-                scores = lax.dot_general(
-                    q_ref[rows, lanes], key, (((1,), (1,)), ((), ())),
-                    preferred_element_type=jnp.float32,
-                ) + bias_rows[a]
-                top = jnp.max(scores, axis=1, keepdims=True)
+                scores = raw[rows] + bias_rows[a]
+                top = jnp.broadcast_to(jnp.max(scores, axis=1, keepdims=True), (BLK, HD))
                 if not first:
-                    before = peak[h, rows, 0:1]
+                    before = peak[h, rows, :]
                     top = jnp.maximum(before, top)
-                weight = jnp.exp2((scores - top) * factor)
-                summed = jnp.sum(weight, axis=1, keepdims=True)
-                product = jnp.dot(
-                    weight.astype(jnp.bfloat16), value, preferred_element_type=jnp.float32
-                )
-                if not first:
-                    fade = jnp.exp2((before - top) * factor)
-                    summed = summed + total[h, rows, 0:1] * fade
-                    product = product + acc[rows, lanes] * fade
-                peak[h, rows, :] = jnp.broadcast_to(top, (BLK, HD))
-                total[h, rows, :] = jnp.broadcast_to(summed, (BLK, HD))
-                acc[rows, lanes] = product
+                    fades.append(jnp.exp2((before - top) * factor))
+                peak[h, rows, :] = top
+                wide_top = jnp.concatenate([top] * len(blocks), axis=1)
+                weights_of.append(jnp.exp2((scores - wide_top) * factor).astype(jnp.bfloat16))
+            product = jnp.dot(
+                jnp.concatenate(weights_of, axis=0),
+                jnp.concatenate([value, ones], axis=1),
+                preferred_element_type=jnp.float32,
+            )
+            if not first:
+                fade = jnp.concatenate(fades, axis=0)
+                product = product + acc[h] * jnp.concatenate([fade, fade], axis=1)
+            acc[h] = product
 
     for copy in own:
         copy.wait()
-    attend(ctx, True)
-
-    def value_relay(j):
+    attend(ctx, (0, 1), True)
+
+    def row_first_relay(j):
         peer = row_peer(j)
         dest = jnp.where(peer > ctx, ctx + reach, ctx - reach)
-        copy = pltpu.make_async_remote_copy(
-            src_ref=kv.at[peer - ctx + reach, V],
-            dst_ref=kv.at[peer - dest + reach, V],
-            send_sem=relay_send.at[peer - ctx + reach, V],
-            recv_sem=kv_recv.at[peer - dest + reach, V],
+        return inside(dest), Pair(lambda kind: pltpu.make_async_remote_copy(
+            src_ref=kv.at[peer - ctx + reach, ROW_FIRST * 2 + kind],
+            dst_ref=kv.at[peer - dest + reach, ROW_FIRST * 2 + kind],
+            send_sem=relay_send.at[peer - ctx + reach, ROW_FIRST * 2 + kind],
+            recv_sem=kv_recv.at[peer - dest + reach, ROW_FIRST * 2 + kind],
             device_id=(dest, t),
             device_id_type=MESH,
-        )
-        return inside(dest), copy
-
-    def key_relay(j):
+        ))
+
+    def outer_first_relay(j):
         peer = row_peer(j)
         src = jnp.where(peer < ctx, ctx - reach, ctx + reach)
-        copy = pltpu.make_async_remote_copy(
-            src_ref=kv.at[src - ctx + reach, K],
-            dst_ref=kv.at[src - peer + reach, K],
-            send_sem=relay_send.at[peer - ctx + reach, K],
-            recv_sem=kv_recv.at[src - peer + reach, K],
+        return inside(src), Pair(lambda kind: pltpu.make_async_remote_copy(
+            src_ref=kv.at[src - ctx + reach, OUTER_FIRST * 2 + kind],
+            dst_ref=kv.at[src - peer + reach, OUTER_FIRST * 2 + kind],
+            send_sem=relay_send.at[peer - ctx + reach, OUTER_FIRST * 2 + kind],
+            recv_sem=kv_recv.at[src - peer + reach, OUTER_FIRST * 2 + kind],
             device_id=(peer, t),
             device_id_type=MESH,
-        )
-        return inside(src), copy
+        ))
 
     def start_relay(make, j):
         valid, copy = make(j)
@@ -196,25 +225,29 @@
         def _():
             copy.wait_send()
 
-    def take_values(j):
-        wait_piece(row_peer(j), V)
-        start_relay(value_relay, j)
-
-    each_peer(take_values)
-    outer(lambda src: wait_piece(src, K))
-    each_peer(lambda j: start_relay(key_relay, j))
+    def pass_row(j):
+        wait_piece(row_peer(j), ROW_FIRST)
+        start_relay(row_first_relay, j)
+
+    each_peer(pass_row)
+    outer(lambda src: wait_piece(src, OUTER_FIRST))
+    each_peer(lambda j: start_relay(outer_first_relay, j))
+    each_peer(lambda j: attend(row_peer(j), (ROW_FIRST,)))
+    outer(lambda src: attend(src, (OUTER_FIRST,)))
 
     def take_row(j):
-        wait_piece(row_peer(j), K)
-        attend(row_peer(j), False)
+        wait_piece(row_peer(j), OUTER_FIRST)
+        attend(row_peer(j), (OUTER_FIRST,))
 
     each_peer(take_row)
 
     def take_outer(src):
-        wait_piece(src, V)
-        attend(src, False)
+        wait_piece(src, ROW_FIRST)
+        attend(src, (ROW_FIRST,))
 
     outer(take_outer)
+    for copy in weights:
+        copy.wait()
 
     def take_diagonal(j):
         peer = row_peer(j)
@@ -222,17 +255,15 @@
 
         @pl.when(inside(src))
         def _():
-            wait_piece(src, K)
-            wait_piece(src, V)
-            attend(src, False)
+            wait_piece(src, OUTER_FIRST)
+            wait_piece(src, ROW_FIRST)
+            attend(src, (0, 1))
 
     each_peer(take_diagonal)
 
     for h in range(heads):
         lanes = slice(h * HD, (h + 1) * HD)
-        att[:, lanes] = (acc[:, lanes] * (1.0 / total[h])).astype(jnp.bfloat16)
-    for copy in weights:
-        copy.wait()
+        att[:, lanes] = (acc[h, :, :HD] * (1.0 / acc[h, :, HD:])).astype(jnp.bfloat16)
 
     def project(slab, k):
         return jnp.dot(
@@ -294,12 +325,12 @@
             result = result + recv_y[jy, k].astype(jnp.float32)
         out_ref[:, k * width:(k + 1) * width] = result.astype(jnp.bfloat16)
 
-    each_peer(lambda j: own_copy(row_peer(j), V).wait_send())
-    each_peer(lambda j: own_copy(row_peer(j), K).wait_send())
-    outer(lambda dest: own_copy(dest, K).wait_send())
-    outer(lambda dest: own_copy(dest, V).wait_send())
-    each_peer(lambda j: end_relay(value_relay, j))
-    each_peer(lambda j: end_relay(key_relay, j))
+    each_peer(lambda j: own_copy(row_peer(j), ROW_FIRST).wait_send())
+    each_peer(lambda j: own_copy(row_peer(j), OUTER_FIRST).wait_send())
+    outer(lambda dest: own_copy(dest, OUTER_FIRST).wait_send())
+    outer(lambda dest: own_copy(dest, ROW_FIRST).wait_send())
+    each_peer(lambda j: end_relay(row_first_relay, j))
+    each_peer(lambda j: end_relay(outer_first_relay, j))
     for jy in range(chips):
         for k in range(chunks):
             partner_copy(jy, k).wait_send()
@@ -320,6 +351,8 @@
     bf16, f32 = jnp.bfloat16, jnp.float32
     dma = pltpu.SemaphoreType.DMA
     slots = 2 * reach + 1
+    held = 2 * (slots * 2 * tok * cols + tp_count * depth * out_cols + 4 * tok * out_cols * chips)
+    held += 4 * tok * (5 * cols + 3 * out_cols)
     return pl.pallas_call(
         functools.partial(kernel, reach, count, tp_count, chunks),
         out_shape=jax.ShapeDtypeStruct((tok, out_cols), bf16),
@@ -332,10 +365,9 @@
         ],
         out_specs=pl.BlockSpec(memory_space=pltpu.VMEM),
         scratch_shapes=[
-            pltpu.VMEM((slots, 2, tok, cols), bf16),
+            pltpu.VMEM((slots, 4, tok // 2, cols), bf16),
             pltpu.VMEM((tp_count, depth, out_cols), bf16),
-            pltpu.VMEM((tok, cols), f32),
-            pltpu.VMEM((heads, tok, HD), f32),
+            pltpu.VMEM((heads, tok, 2 * HD), f32),
             pltpu.VMEM((heads, tok, HD), f32),
             pltpu.VMEM((tok, cols), bf16),
             pltpu.VMEM((chips, chunks, tok, width), bf16),
@@ -343,11 +375,11 @@
             pltpu.VMEM((chips, chunks, tok, width), bf16),
             pltpu.VMEM((chips, chunks, tok, width), bf16),
             pltpu.VMEM((chunks, tok, width), f32),
-            dma((2,)),
+            dma((4,)),
             dma((tp_count,)),
-            dma((slots, 2)),
-            dma((slots, 2)),
-            dma((slots, 2)),
+            dma((slots, 4)),
+            dma((slots, 4)),
+            dma((slots, 4)),
             dma((chips, chunks)),
             dma((chips, chunks)),
             dma((chips, chunks)),

time: 55.5 us -> 49.1 us (0.88)
  Pallas kernels: 53.3 us -> 46.9 us
    pallas_call x1, Pallas kernels: 53.3 us -> 46.9 us  [shards(): pl.pallas_call(functools.partial(kernel, reach, count, tp_count, chunks),...]
where the time goes in v2:
time: 49.1 us; the launch traced here: 48.8 us
  Pallas kernels  46.9 us (96%)
  local copies, waits for them, and re-layouts  1.97 us (4%)
    pallas_call x1, Pallas kernels, shards(): pl.pallas_call(functools.partial(kernel, reach, count, tp_count, chunks),...  46.9 us
    unnamed x1, local copies, waits for them, and re-layouts  1.97 us

profile of v2, /device:TPU:16, one launch (start us, length us, event | category | flops | bytes accessed | tf_op | source)
XLA Modules:
  0.0 48.8 jit_solution(2196115009362813002)
XLA Ops:
  0.0 46.9 %shard_map.55 = bf16[256,1280]{1,0:T(8,128)(2,1)} custom-call(s32[16,16]{1,0:T(8,128)} %mask_ref.1, bf16[256,640]{1,0:T(8,128)(2,1)} %q_ref.1, bf16[256,640]{1,0:T(8,128)(2,1)} %k_ref.1, bf16[256,640]{1,0:T(8,128)(2,1)} %v_ref.1, bf16[640,5120]{1,0:T(8,128)(2,1)} %w_ref.1), custom_call_target="tpu_custom_call" | custom-call | tf_op jit(solution)/shard_map/pallas_call | solution.py:356
  46.9 2.0 %copy.7 = bf16[256,1280]{1,0:T(8,128)(2,1)} copy(bf16[256,1280]{1,0:T(8,128)(2,1)} %shard_map.55) | data formatting | bytes 1310720

commit v3 on v2

--- a/solution.py
+++ b/solution.py
@@ -17,15 +17,15 @@
 
 def kernel(
     reach, count, tp_count, chunks,
-    mask_ref, q_ref, k_ref, v_ref, w_ref, out_ref,
-    kv, w_vm, acc, peak, att, stage_p, recv_p, stage_y, recv_y, final,
-    kv_local, w_local, own_send, relay_send, kv_recv, p_send, p_recv, y_send, y_recv,
+    mask_ref, q_ref, k_ref, v_ref, w_ref, near_ref, far_ref,
+    kv, w_vm, acc, peak, att, stage_p, recv_p, stage_y, final,
+    kv_local, w_local, own_send, relay_send, kv_recv, p_send, p_recv, y_send, y_recv, near_sem,
 ):
     tok, cols = q_ref.shape
     heads = cols // HD
     per = tok // BLK
     chips = tp_count // 2
-    out_cols = out_ref.shape[1]
+    out_cols = near_ref.shape[1]
     width = out_cols // chunks
     ctx = lax.axis_index("ctx")
     t = lax.axis_index("tp")
@@ -284,11 +284,16 @@
     def chip_copy(jy, k):
         return pltpu.make_async_remote_copy(
             src_ref=stage_y.at[jy, k],
-            dst_ref=recv_y.at[chips - jy, k],
+            dst_ref=far_ref.at[chips - jy - 1, :, k * width:(k + 1) * width],
             send_sem=y_send.at[jy, k],
             recv_sem=y_recv.at[chips - jy, k],
             device_id=(ctx, tp_of(jy, core)),
             device_id_type=MESH,
+        )
+
+    def near_copy(k):
+        return pltpu.make_async_copy(
+            final.at[k], near_ref.at[:, k * width:(k + 1) * width], near_sem.at[k]
         )
 
     pending = []
@@ -300,16 +305,24 @@
             pending.append(copy)
 
     for jy in range(1, chips):
-        for k in range(chunks):
-            stage_p[jy, k] = project(tp_of(jy, 1 - core), k).astype(jnp.bfloat16)
-            push(partner_copy(jy, k))
-    for jy in range(1, chips):
-        for k in range(chunks):
-            mine = project(tp_of(jy, core), k)
-            push(None)
-            partner_copy(jy, k).wait_recv()
-            stage_y[jy, k] = (mine + recv_p[jy, k].astype(jnp.float32)).astype(jnp.bfloat16)
-            push(chip_copy(jy, k))
+        there, here = tp_of(jy, 1 - core), tp_of(jy, core)
+        for step in range(chunks + 1):
+            if step < chunks:
+                @pl.when(t >= 0)
+                def _():
+                    stage_p[jy, step] = project(there, step).astype(jnp.bfloat16)
+                push(partner_copy(jy, step))
+            if step > 0:
+                k = step - 1
+                if step == chunks:
+                    push(None)
+                partner_copy(jy, k).wait_recv()
+
+                @pl.when(t >= 0)
+                def _():
+                    mine = project(here, k) + recv_p[jy, k].astype(jnp.float32)
+                    stage_y[jy, k] = mine.astype(jnp.bfloat16)
+                push(chip_copy(jy, k))
     for k in range(chunks):
         stage_p[0, k] = project(tp_of(0, 1 - core), k).astype(jnp.bfloat16)
         push(partner_copy(0, k))
@@ -318,12 +331,12 @@
         push(None)
         partner_copy(0, k).wait_recv()
         final[k] = mine + recv_p[0, k].astype(jnp.float32)
+        push(near_copy(k))
+    push(None)
     for k in range(chunks):
-        result = final[k]
         for jy in range(1, chips):
             chip_copy(chips - jy, k).wait_recv()
-            result = result + recv_y[jy, k].astype(jnp.float32)
-        out_ref[:, k * width:(k + 1) * width] = result.astype(jnp.bfloat16)
+        near_copy(k).wait()
 
     each_peer(lambda j: own_copy(row_peer(j), ROW_FIRST).wait_send())
     each_peer(lambda j: own_copy(row_peer(j), OUTER_FIRST).wait_send())
@@ -351,11 +364,12 @@
     bf16, f32 = jnp.bfloat16, jnp.float32
     dma = pltpu.SemaphoreType.DMA
     slots = 2 * reach + 1
-    held = 2 * (slots * 2 * tok * cols + tp_count * depth * out_cols + 4 * tok * out_cols * chips)
-    held += 4 * tok * (5 * cols + 3 * out_cols)
-    return pl.pallas_call(
+    near, far = pl.pallas_call(
         functools.partial(kernel, reach, count, tp_count, chunks),
-        out_shape=jax.ShapeDtypeStruct((tok, out_cols), bf16),
+        out_shape=[
+            jax.ShapeDtypeStruct((tok, out_cols), f32),
+            jax.ShapeDtypeStruct((chips - 1, tok, out_cols), bf16),
+        ],
         in_specs=[
             pl.BlockSpec(memory_space=pltpu.SMEM),
             pl.BlockSpec(memory_space=pltpu.VMEM),
@@ -363,14 +377,13 @@
             pl.BlockSpec(memory_space=pl.ANY),
             pl.BlockSpec(memory_space=pl.ANY),
         ],
-        out_specs=pl.BlockSpec(memory_space=pltpu.VMEM),
+        out_specs=[pl.BlockSpec(memory_space=pl.ANY)] * 2,
         scratch_shapes=[
             pltpu.VMEM((slots, 4, tok // 2, cols), bf16),
             pltpu.VMEM((tp_count, depth, out_cols), bf16),
             pltpu.VMEM((heads, tok, 2 * HD), f32),
             pltpu.VMEM((heads, tok, HD), f32),
             pltpu.VMEM((tok, cols), bf16),
-            pltpu.VMEM((chips, chunks, tok, width), bf16),
             pltpu.VMEM((chips, chunks, tok, width), bf16),
             pltpu.VMEM((chips, chunks, tok, width), bf16),
             pltpu.VMEM((chips, chunks, tok, width), bf16),
@@ -384,11 +397,15 @@
             dma((chips, chunks)),
             dma((chips, chunks)),
             dma((chips, chunks)),
+            dma((chunks,)),
         ],
         compiler_params=pltpu.CompilerParams(
             collective_id=0, has_side_effects=True, vmem_limit_bytes=60 * 1024 * 1024
         ),
     )(block_mask, queries, keys, values, w_out)
+    for other in range(chips - 1):
+        near = near + far[other].astype(f32)
+    return near.astype(bf16)
 
 
 def solution(mesh):

time: 49.1 us -> 48.5 us (0.988)
  other arithmetic: 0 us -> 2.43 us
  local copies, waits for them, and re-layouts: 1.97 us -> 0 us
  Pallas kernels: 46.9 us -> 45.4 us
    convert_element_type x0 -> x1, other arithmetic: none -> 2.43 us  [shards(): return near.astype(bf16)]
    unnamed x1 -> x0, local copies, waits for them, and re-layouts: 1.97 us -> none
    pallas_call x1, Pallas kernels: 46.9 us -> 45.4 us  [shards(): pl.pallas_call(functools.partial(kernel, reach, count, tp_count, chunks),...]
where the time goes in v3:
time: 48.5 us; the launch traced here: 47.8 us
  Pallas kernels  45.4 us (94%)
  other arithmetic  2.43 us (5%)
    pallas_call x1, Pallas kernels, shards(): pl.pallas_call(functools.partial(kernel, reach, count, tp_count, chunks),...  45.4 us
    convert_element_type x1, other arithmetic, shards(): return near.astype(bf16)  2.43 us

profile of v3, /device:TPU:16, one launch (start us, length us, event | category | flops | bytes accessed | tf_op | source)
XLA Modules:
  0.0 47.8 jit_solution(12919618478712842129)
XLA Ops:
  0.0 45.4 %shard_map.55 = (f32[256,1280]{1,0:T(8,128)}, bf16[1,256,1280]{2,1,0:T(8,128)(2,1)}) custom-call(s32[16,16]{1,0:T(8,128)} %mask_ref.1, bf16[256,640]{1,0:T(8,128)(2,1)} %q_ref.1, bf16[256,640]{1,0:T(8,128)(2,1)} %k_ref.1, bf16[256,640]{1,0:T(8,128)(2,1)} %v_ref.1, bf16[640,5120]{1,0:T(8,128)(2,1)} %w_ref.1), custom_call_target="tpu_custom_call" | custom-call | tf_op jit(solution)/shard_map/pallas_call | solution.py:367
  45.4 2.4 %fusion = bf16[256,1280]{1,0:T(8,128)(2,1)} fusion(f32[256,1280]{1,0:T(8,128)} %get-tuple-element.7, bf16[1,256,1280]{2,1,0:T(8,128)(2,1)} %get-tuple-element.8), kind=kLoop, calls=%fused_computation.1 | loop fusion | flops 983040 | bytes 2621440 | tf_op jit(solution)/shard_map/convert_element_type | solution.py:408
